TPU v7x, 768 devices: a whole 4x8x12 slice. The times are simulated.
768 devices in a mesh: lon: 64 (over x, z_hi, y), lat: 12 (over z_lo, core).
Axes of the slice: x: 4, y: 8, z: 12 (z_hi: 2, z_lo: 6; z = z_hi * 6 + z_lo), core: 2. Of those that a mesh axis runs over, the one named last changes fastest.
Arguments:
- fields: bfloat16 [180, 641, 768], P('lat', None, 'lon'), may hold values from -6 to 6
- support: int32 [180, 5], replicated, may hold values from 1 to 48, as said below
- filter_weight: bfloat16 [641, 4], replicated, may hold values from -4 to 4
- w_up: bfloat16 [641, 1282], replicated, may hold values from -0.25 to 0.25
- w_down: bfloat16 [1282, 641], replicated, may hold values from -0.15625 to 0.15625
Outputs:
- result: bfloat16 [180, 641, 768], P('lat', None, 'lon')
Inputs may be any that keep to these rules, and one draw needn't show every extreme that they name: support[o, j] is the half-width in longitude cells of the filter's support at output latitude o and latitude offset j - 2; the value 48 occurs.
All inputs are finite; a program needn't handle non-finite values.
Results may differ from a plain program's by a relative error of at most 0.0085.
Values may be sent and summed in bfloat16 or wider, within the bound.
A program may use at most 64 MiB of HBM per device.

v0:
```python
import functools
import math

import jax
import jax.numpy as jnp
import numpy as np
from jax import lax
from jax.experimental import pallas as pl
from jax.experimental.pallas import tpu as pltpu
from jax.sharding import PartitionSpec as P

MESH = pl.DeviceIdType.MESH
NB = 12
ROWS = 15
C = 641
CH = 10
OWN = 64
K = 4
R = 2
F32 = jnp.float32
BF = jnp.bfloat16


def iota(shape, dim):
    return lax.broadcasted_iota(jnp.int32, shape, dim)


def pack(f_ref, o_ref, roll_ref):
    lane = iota((16, 128), 1)
    sub = iota((16, 128), 0)
    for n in range(NB):
        x = f_ref[n].astype(F32)
        x = jnp.concatenate([x, jnp.zeros((ROWS, 768 - C), F32)], axis=1)
        x = jnp.concatenate([x, jnp.zeros((1, 768), F32)], axis=0)
        roll_ref[n] = pltpu.roll(x, CH * n, 1) if n else x
    extra = jnp.zeros((16, 128), F32)
    spread = jnp.zeros((16, 128), F32)
    for n in range(NB):
        start = 640 + CH * n
        col = roll_ref[n, :, pl.ds(start % 768, 1)] if start < 768 else None
        if col is None:
            col = roll_ref[n, :, pl.ds(start - 768, 1)]
        col = jnp.broadcast_to(col, (16, 128))
        if n < 8:
            extra = jnp.where(lane == 120 + n, col, extra)
        else:
            spread = jnp.where(lane == 8 * sub + (n - 8), col, spread)
    spread = jnp.where(sub < ROWS, spread, 0.0)
    last = jnp.sum(spread, axis=0, keepdims=True)
    for p in range(OWN):
        begin = CH * p
        cut = begin % 128
        tile = begin // 128
        here = (lane - cut) & 127
        acc = jnp.zeros((16, 128), F32)
        for n in range(NB):
            lo, hi = begin + CH * n, begin + CH * n + CH
            inside = (here >= CH * n) & (here < CH * n + CH)
            first, final = lo // 128, (hi - 1) // 128
            acc = jnp.where(inside, roll_ref[n, :, pl.ds(first % 6 * 128, 128)], acc) if first == final else jnp.where(
                inside,
                jnp.where(
                    lane >= 64,
                    roll_ref[n, :, pl.ds(first % 6 * 128, 128)],
                    roll_ref[n, :, pl.ds(final % 6 * 128, 128)],
                ),
                acc,
            )
        if cut:
            acc = pltpu.roll(acc, 128 - cut, 1)
        acc = jnp.where(lane >= 120, extra, acc)
        acc = jnp.where(sub == 15, last, acc)
        o_ref[p] = acc.astype(BF)


def unpack(m_ref, c_ref, turn_ref):
    lane = iota((16, 128), 1)
    sub = iota((16, 128), 0)
    for q in range(OWN):
        x = m_ref[q].astype(F32)
        cut = (CH * q) % 128
        turn_ref[q] = pltpu.roll(x, cut, 1) if cut else x
    x0 = m_ref[0].astype(F32)
    row = jnp.broadcast_to(x0[15:16], (16, 128))
    lane1 = iota((16, 128), 1)
    for n in range(NB):
        tiles = []
        for t in range(6):
            acc = jnp.zeros((16, 128), F32)
            for q in range(OWN):
                for lo in (CH * (q + n), CH * (q + n) - 768):
                    a, b = max(lo, t * 128) - t * 128, min(lo + CH, t * 128 + 128) - t * 128
                    if a < b:
                        acc = jnp.where((lane1 >= a) & (lane1 < b), turn_ref[q], acc)
            tiles.append(acc)
        full = jnp.concatenate(tiles, axis=1)
        if n:
            full = pltpu.roll(full, 768 - CH * n, 1)
        if n < 8:
            col = x0[:, 120 + n : 121 + n]
        else:
            col = jnp.sum(jnp.where(lane == 8 * sub + (n - 8), row, 0.0), axis=1, keepdims=True)
        c_ref[pl.ds(16 * n, 16), pl.ds(0, 640)] = full[:, :640]
        c_ref[pl.ds(16 * n, 16), pl.ds(640, 128)] = jnp.where(lane == 0, col, 0.0)


def order_matrix():
    j = np.arange(128)
    g, s = j // 24, j % 24
    c = 2 * g + np.where(s < 8, 0, np.where(s < 16, 1, np.where(s < 20, 0, 1)))
    n = np.where(s < 8, s, np.where(s < 16, s - 8, np.where(s < 20, s - 8, s - 12)))
    src = np.where(j < 120, CH * n + c, j)
    return (src[:, None] == np.arange(128)[None, :]).astype(np.float32)


def back_matrix():
    out = np.zeros((96, 256), np.float32)
    for g in range(5):
        for s in range(16):
            if s < 12:
                out[16 * g + s, CH * s + 2 * g] = 1
            if s < 8 or s >= 12:
                n = s if s < 8 else s - 4
                out[16 * g + s, 128 + CH * n + 2 * g + 1] = 1
    for s in range(8):
        out[80 + s, 120 + s] = 1
    return out


def last_matrix():
    out = np.zeros((256, 128), np.float32)
    for o in range(ROWS):
        for t in range(4):
            out[16 * o + 8 + t, 8 * o + t] = 1
    return out


def sines():
    i = np.arange(192, dtype=np.float64) - R
    return np.sin(np.pi * (i + 0.5) / 180.0).astype(np.float32)[None]


def build_weights(sup_ref, sin_ref, start, t_ref):
    lane = iota((16, 128), 1)
    rlane = lane // 16
    s = lane % 16
    n_in = jnp.where(s < 12, s, s - 4)
    sub = iota((16, 128), 0)
    n_out = jnp.where(sub < 12, sub, sub - 4)
    diff = (n_in - n_out).astype(F32)

    def one(o, carry):
        local = o % 4
        group = o // 4
        row = jnp.minimum(start + o, 179)
        d = rlane - local
        width = jnp.ones((16, 128), F32)
        sine = jnp.zeros((16, 128), F32)
        for j in range(2 * R + 1):
            width = jnp.where(d == j, sup_ref[j, row].astype(F32), width)
            sine = jnp.where(d == j, sin_ref[0, row + j], sine)
        ok = (d >= 0) & (d <= 2 * R)
        scale = jnp.where(ok, sine / jnp.sqrt((2.0 * R + 1.0) * (2.0 * width + 1.0)), 0.0)
        lat = (d - R).astype(F32) / (R + 1.0)
        lat2 = lat * lat
        base = pl.multiple_of(local * 64, 64)
        for step in range(9):
            m = diff + float(12 * (step - 4))
            lon = m / (width + 1.0)
            radius = jnp.sqrt(lat2 + lon * lon) * (K - 1.0)
            w = jnp.where(jnp.abs(m) <= width, scale, 0.0)
            for k in range(K):
                hat = jnp.maximum(0.0, 1.0 - jnp.abs(radius - float(k)))
                t_ref[group, pl.ds(base + 16 * k, 16), pl.ds(128 * step, 128)] = (hat * w).astype(BF)
        return carry

    lax.fori_loop(0, 16, one, 0)


def build_filter(filt_ref, me, w_ref):
    lane = iota((C, 768), 1)
    chan = lane // 64
    want = jnp.where(chan < CH, me * CH + chan, C - 1)
    pick = jnp.where(iota((C, 768), 0) == want, 1.0, 0.0).astype(BF)
    w_ref[...] = jnp.dot(filt_ref[...], pick, preferred_element_type=F32)


NT = (((1,), (1,)), ((), ()))
TN = (((0,), (0,)), ((), ()))


def spread_rows(order_ref, own_ref, up_ref, down_ref, lat, lats, x_ref, d_ref, e_ref, f_ref):
    lane8 = iota((8, 128), 1)
    sub8 = iota((8, 128), 0)
    left = lane8 < 64
    both = (sub8 < 4) == left
    corner = (sub8 < 4) & left
    eye = (iota((128, 128), 0) == iota((128, 128), 1)).astype(F32).astype(BF)
    order = order_ref[...]

    def load(which, rows, first, keep):
        def rowsof(r):
            x = x_ref[pl.ds(r, 64, stride=16), :]
            if keep is not None:
                x = jnp.where(keep, x, 0.0)
            x = x.astype(BF)
            return jnp.concatenate([x, x], axis=0)

        x_ref[...] = which[...].reshape(1024, 128).astype(F32)
        ex = lax.dot_general(eye, rowsof(15), NT, preferred_element_type=F32)
        for i, r in enumerate(rows):
            d_ref[first + i] = lax.dot_general(order, rowsof(r), NT, preferred_element_type=F32)
            e_ref[first + i] = ex[8 * r : 8 * r + 8]

    load(own_ref, range(ROWS), R, None)
    load(up_ref, (13, 14), 0, lat > 0)
    load(down_ref, (0, 1), ROWS + R, lat < lats - 1)
    for step in range(9):
        f_ref[step, pl.ds(304, 16), :] = jnp.zeros((16, 768), BF)

    def one(r, carry):
        at = pl.multiple_of(16 * r, 16)
        for step in range(9):
            shift = (4 - step) % 128
            turned = d_ref[r]
            ex = e_ref[r]
            if shift:
                turned = pltpu.roll(turned, shift, 1)
                ex = pltpu.roll(ex, shift, 1)
            for g in range(6):
                if g < 5:
                    top = jnp.where(left, turned[24 * g : 24 * g + 8], turned[24 * g + 8 : 24 * g + 16])
                    low = jnp.where(both, turned[24 * g + 16 : 24 * g + 24], 0.0)
                else:
                    top = jnp.where(left, turned[120:128], 0.0)
                    low = jnp.where(corner, ex, 0.0)
                f_ref[step, pl.ds(at, 16), pl.ds(128 * g, 128)] = jnp.concatenate([top, low], axis=0).astype(BF)
        return carry

    lax.fori_loop(0, ROWS + 2 * R, one, 0)


def convolve(t_ref, f_ref, w_ref, back_ref, final_ref, acc_ref, x_ref, z_ref, out_ref):
    def group(g, carry):
        at = pl.multiple_of(64 * g, 64)
        for j in range(3):
            rhs = jnp.concatenate([f_ref[step, pl.ds(at, 128), pl.ds(256 * j, 256)] for step in range(9)], axis=0)
            acc_ref[:, pl.ds(256 * j, 256)] = jnp.dot(t_ref[g], rhs, preferred_element_type=F32)
        for o in range(4):
            conv = jnp.zeros((16, 768), F32)
            for k in range(K):
                conv = conv + acc_ref[pl.ds(64 * o + 16 * k, 16), :] * w_ref[pl.ds(k, 1), :]
            centre = f_ref[4, pl.ds(at + 16 * (o + R), 16), :].astype(F32)
            comb = (centre + conv).astype(BF)
            stack = jnp.concatenate([comb[:, 128 * i : 128 * i + 128] for i in range(6)], axis=0)
            moved = lax.dot_general(stack, back_ref[...], TN, preferred_element_type=F32)
            x_ref[pl.ds(4 * g + o, 64, stride=16), :] = moved[:64, :128] + moved[64:, 128:]
            z_ref[pl.ds(at + 16 * o, 16), :] = comb[:, 640:]
        return carry

    lax.fori_loop(0, 4, group, 0)
    last = lax.dot_general(z_ref[...], final_ref[...], TN, preferred_element_type=F32)
    x_ref[pl.ds(15, 64, stride=16), :] = last[:64]
    out_ref[...] = x_ref[...].reshape(64, 16, 128).astype(BF)


def mlp(c_ref, up_ref, down_ref, out_ref):
    lane = iota((192, 768), 1)
    values = c_ref[...]
    mean = jnp.sum(values, axis=1, keepdims=True) * (1.0 / C)
    centered = jnp.where(lane < C, values - mean, 0.0)
    spread = jnp.sum(centered * centered, axis=1, keepdims=True) * (1.0 / C)
    normed = (centered * lax.rsqrt(spread + 1e-05)).astype(BF)[:, :C]
    raised = jnp.dot(normed, up_ref[...], preferred_element_type=F32)
    hidden = (0.5 * raised * (1.0 + lax.erf(raised * math.sqrt(0.5)))).astype(BF)
    lowered = lax.dot_general(hidden, down_ref[...], NT, preferred_element_type=F32)
    result = (values[:, :C] + lowered).astype(BF)
    for n in range(NB):
        out_ref[n] = result[16 * n : 16 * n + ROWS]


def pack_kernel(f_ref, o_ref, roll_ref):
    pack(f_ref, o_ref, roll_ref)


def conv_kernel(lats, own_ref, up_ref, down_ref, sup_ref, sin_ref, filt_ref, order_ref, back_ref, final_ref, out_ref,
                t_ref, w_ref, x_ref, d_ref, e_ref, f_ref, acc_ref, z_ref):
    me = lax.axis_index("lon")
    lat = lax.axis_index("lat")
    build_weights(sup_ref, sin_ref, lat * ROWS, t_ref)
    build_filter(filt_ref, me, w_ref)
    spread_rows(order_ref, own_ref, up_ref, down_ref, lat, lats, x_ref, d_ref, e_ref, f_ref)
    convolve(t_ref, f_ref, w_ref, back_ref, final_ref, acc_ref, x_ref, z_ref, out_ref)


def mlp_kernel(m_ref, up_ref, down_ref, out_ref, turn_ref, c_ref):
    unpack(m_ref, c_ref, turn_ref)
    mlp(c_ref, up_ref, down_ref, out_ref)


def greet(me, lat, lats, halo):
    barrier = pltpu.get_barrier_semaphore()

    def hail(i, carry):
        pl.semaphore_signal(barrier, inc=1, device_id={"lon": lax.rem(me + i, OWN)}, device_id_type=MESH)
        return carry

    lax.fori_loop(1, OWN, hail, 0)
    if not halo:
        pl.semaphore_wait(barrier, OWN - 1)
        return

    @pl.when(lat > 0)
    def _():
        pl.semaphore_signal(barrier, inc=1, device_id={"lat": lat - 1}, device_id_type=MESH)

    @pl.when(lat < lats - 1)
    def _():
        pl.semaphore_signal(barrier, inc=1, device_id={"lat": lat + 1}, device_id_type=MESH)

    pl.semaphore_wait(barrier, OWN - 1 + (lat > 0).astype(jnp.int32) + (lat < lats - 1).astype(jnp.int32))


def exchange(me, src, dst, send_sem, recv_sem, copy_sem):
    def send(i, carry):
        p = lax.rem(me + i, OWN)
        pltpu.make_async_remote_copy(
            src.at[p], dst.at[me], send_sem, recv_sem, device_id={"lon": p}, device_id_type=MESH
        ).start()
        return carry

    lax.fori_loop(1, OWN, send, 0)
    mine = pltpu.make_async_copy(src.at[me], dst.at[me], copy_sem)
    mine.start()
    mine.wait()
    every = pltpu.make_async_remote_copy(
        src.at[pl.ds(0, OWN - 1)], dst.at[pl.ds(0, OWN - 1)], send_sem, recv_sem,
        device_id={"lon": lax.rem(me + 1, OWN)}, device_id_type=MESH,
    )
    every.wait_recv()
    every.wait_send()


def first_exchange(lats, src, own, up, down, send_sem, recv_sem, copy_sem, halo_send, halo_recv):
    me = lax.axis_index("lon")
    lat = lax.axis_index("lat")
    greet(me, lat, lats, True)
    exchange(me, src, own, send_sem, recv_sem, copy_sem)

    def halo(to, dst, i):
        return pltpu.make_async_remote_copy(
            own, dst, halo_send.at[i], halo_recv.at[i], device_id={"lat": to}, device_id_type=MESH
        )

    @pl.when(lat > 0)
    def _():
        halo(lat - 1, down, 0).start()

    @pl.when(lat < lats - 1)
    def _():
        halo(lat + 1, up, 1).start()

    @pl.when(lat > 0)
    def _():
        halo(lat - 1, down, 0).wait_send()
        halo(lat - 1, up, 1).wait_recv()

    @pl.when(lat < lats - 1)
    def _():
        halo(lat + 1, up, 1).wait_send()
        halo(lat + 1, down, 0).wait_recv()


def second_exchange(src, own, send_sem, recv_sem, copy_sem):
    me = lax.axis_index("lon")
    greet(me, None, None, False)
    exchange(me, src, own, send_sem, recv_sem, copy_sem)


VM = pl.BlockSpec(memory_space=pltpu.VMEM)
SM = pl.BlockSpec(memory_space=pltpu.SMEM)
MSG = jax.ShapeDtypeStruct((OWN, 16, 128), BF)


def params(**kw):
    return pltpu.CompilerParams(vmem_limit_bytes=48 << 20, **kw)


def on_device(lats, fields, support, filter_weight, w_up, w_down):
    points = jnp.transpose(fields, (2, 0, 1))
    messages = pl.pallas_call(
        pack_kernel, out_shape=MSG, in_specs=[VM], out_specs=VM,
        scratch_shapes=[pltpu.VMEM((NB, 16, 768), F32)], compiler_params=params(), name="pack",
    )(points)
    dma = pltpu.SemaphoreType.DMA
    own, up, down = pl.pallas_call(
        functools.partial(first_exchange, lats), out_shape=(MSG,) * 3, in_specs=[VM], out_specs=(VM,) * 3,
        scratch_shapes=[dma, dma, dma, dma((2,)), dma((2,))],
        compiler_params=params(collective_id=0, has_side_effects=True), name="to_owners",
    )(messages)
    back = pl.pallas_call(
        functools.partial(conv_kernel, lats), out_shape=MSG,
        in_specs=[VM, VM, VM, SM, SM, VM, VM, VM, VM], out_specs=VM,
        scratch_shapes=[
            pltpu.VMEM((4, 256, 1152), BF), pltpu.VMEM((K, 768), F32), pltpu.VMEM((1024, 128), F32),
            pltpu.VMEM((ROWS + 2 * R, 128, 128), F32), pltpu.VMEM((ROWS + 2 * R, 8, 128), F32),
            pltpu.VMEM((9, 320, 768), BF), pltpu.VMEM((256, 768), F32), pltpu.VMEM((256, 128), BF),
        ],
        compiler_params=params(), name="convolve",
    )(own, up, down, support.T, jnp.asarray(sines()), filter_weight.T, jnp.asarray(order_matrix(), BF),
      jnp.asarray(back_matrix(), BF), jnp.asarray(last_matrix(), BF))
    pieces = pl.pallas_call(
        second_exchange, out_shape=MSG, in_specs=[VM], out_specs=VM, scratch_shapes=[dma, dma, dma],
        compiler_params=params(collective_id=1, has_side_effects=True), name="to_longitudes",
    )(back)
    result = pl.pallas_call(
        mlp_kernel, out_shape=jax.ShapeDtypeStruct((NB, ROWS, C), BF), in_specs=[VM] * 3, out_specs=VM,
        scratch_shapes=[pltpu.VMEM((OWN, 16, 128), F32), pltpu.VMEM((192, 768), F32)],
        compiler_params=params(), name="channels",
    )(pieces, w_up, w_down.T)
    return jnp.transpose(result, (1, 2, 0))


def solution(mesh):
    in_specs = (P("lat", None, "lon"), P(), P(), P(), P())
    out_specs = P("lat", None, "lon")
    return jax.shard_map(
        functools.partial(on_device, mesh.shape["lat"]), mesh=mesh, in_specs=in_specs, out_specs=out_specs,
        check_vma=False,
    )
```

profile of v0, /device:TPU:1, one launch (start us, length us, event | category | flops | bytes accessed | tf_op | source)
XLA Modules:
  0.0 79.9 jit_solution(12934208134420778958)
XLA Ops:
  0.0 0.0 copy-start
  0.0 0.0 copy-start.2
  0.0 1.1 %copy-done.2 = bf16[15,641,12]{1,0,2:T(8,128)(2,1)S(1)} copy-done((bf16[15,641,12]{1,0,2:T(8,128)(2,1)S(1)}, bf16[15,641,12]{1,0,2:T(8,128)(2,1)}, u32[]{:S(2)}) %copy-start.2) | copy-done | bytes 230784
  1.1 0.7 pack.1.src
  1.8 38.1 %to_owners.1 = (bf16[64,16,128]{2,1,0:T(8,128)(2,1)S(1)}, bf16[64,16,128]{2,1,0:T(8,128)(2,1)S(1)}, bf16[64,16,128]{2,1,0:T(8,128)(2,1)S(1)}) custom-call(bf16[64,16,128]{2,1,0:T(8,128)(2,1)S(1)} %pack.1.src), custom_call_target="tpu_custom_call" | custom-call | tf_op jit(solution)/shard_map/to_owners/pallas_call | solution.py:396
  39.8 0.0 copy-start.3
  39.9 0.8 %copy-done.3 = bf16[256,128]{1,0:T(8,128)(2,1)S(1)} copy-done((bf16[256,128]{1,0:T(8,128)(2,1)S(1)}, bf16[256,128]{1,0:T(8,128)(2,1)}, u32[]{:S(2)}) %copy-start.3) | copy-done | bytes 65560
  40.7 0.0 copy-start.4
  40.7 0.8 copy-done.4
  41.5 0.0 copy-start.5
  41.5 0.8 copy-done.5
  42.2 0.0 copy-start.6
  42.2 0.7 copy-done.6
  42.9 0.0 copy-start.7
  42.9 0.7 copy-done.7
  43.6 0.0 copy-start.8
  43.6 0.7 copy-done.8
  44.3 10.5 %convolve.1.src = bf16[64,16,128]{2,1,0:T(8,128)(2,1)S(1)} custom-call(bf16[64,16,128]{2,1,0:T(8,128)(2,1)S(1)} %get-tuple-element.8.own_ref, bf16[64,16,128]{2,1,0:T(8,128)(2,1)S(1)} %get-tuple-element.9.up_ref, bf16[64,16,128]{2,1,0:T(8,128)(2,1)S(1)} %get-tuple-element.10.down_ref, s32[5,180]{1,0:T(8,128)S(1)} %bitcast.7, f32[1,192]{1,0:T(1,128)S(1)} %copy-done.8, ...), custom_call_target="tpu_custom_call" | custom-call | tf_op jit(solution)/shard_map/convolve/pallas_call | solution.py:401
  54.8 20.9 %to_longitudes.1.m_ref = bf16[64,16,128]{2,1,0:T(8,128)(2,1)S(1)} custom-call(bf16[64,16,128]{2,1,0:T(8,128)(2,1)S(1)} %convolve.1.src), custom_call_target="tpu_custom_call" | custom-call | tf_op jit(solution)/shard_map/to_longitudes/pallas_call | solution.py:412
  75.8 0.0 copy-done
  75.8 0.0 copy-start.1
  75.8 1.5 %copy-done.1 = bf16[1282,641]{0,1:T(8,128)(2,1)S(1)} copy-done((bf16[1282,641]{0,1:T(8,128)(2,1)S(1)}, bf16[1282,641]{0,1:T(8,128)(2,1)}, u32[]{:S(2)}) %copy-start.1) | copy-done | bytes 1643548
  77.3 2.6 %channels.1 = bf16[12,15,641]{2,1,0:T(8,128)(2,1)} custom-call(bf16[64,16,128]{2,1,0:T(8,128)(2,1)S(1)} %to_longitudes.1.m_ref, bf16[641,1282]{1,0:T(8,128)(2,1)S(1)} %copy-done, bf16[641,1282]{1,0:T(8,128)(2,1)S(1)} %bitcast.5), custom_call_target="tpu_custom_call" | custom-call | tf_op jit(solution)/shard_map/channels/pallas_call | solution.py:416
Async XLA Ops:
  0.0 75.8 %copy-start = (bf16[641,1282]{1,0:T(8,128)(2,1)S(1)}, bf16[641,1282]{1,0:T(8,128)(2,1)}, u32[]{:S(2)}) copy-start(bf16[641,1282]{1,0:T(8,128)(2,1)} %up_ref.1) | copy-start | bytes 4930576
  0.0 1.1 %copy-start.2 = (bf16[15,641,12]{1,0,2:T(8,128)(2,1)S(1)}, bf16[15,641,12]{1,0,2:T(8,128)(2,1)}, u32[]{:S(2)}) copy-start(bf16[15,641,12]{1,0,2:T(8,128)(2,1)} %param.9) | copy-start | bytes 692284
  39.8 0.8 %copy-start.3 = (bf16[256,128]{1,0:T(8,128)(2,1)S(1)}, bf16[256,128]{1,0:T(8,128)(2,1)}, u32[]{:S(2)}) copy-start(bf16[256,128]{1,0:T(8,128)(2,1)} %constant.11.clone.final_ref) | copy-start | bytes 196612
  40.7 0.8 copy-start.4
  41.5 0.8 copy-start.5
  42.2 0.7 copy-start.6
  42.9 0.7 copy-start.7
  43.6 0.7 copy-start.8
  75.8 1.5 %copy-start.1 = (bf16[1282,641]{0,1:T(8,128)(2,1)S(1)}, bf16[1282,641]{0,1:T(8,128)(2,1)}, u32[]{:S(2)}) copy-start(bf16[1282,641]{0,1:T(8,128)(2,1)} %param.13) | copy-start | bytes 4930576
where the time goes:
time: 80.4 us; the launch traced here: 79.9 us
  Pallas kernels  72.8 us (91%)
  local copies, waits for them, and re-layouts  7.05 us (9%)
    pallas_call x1, Pallas kernels, on_device(): pl.pallas_call(functools.partial(first_exchange, lats), out_shape=(MSG,)...  38.1 us
    pallas_call x1, Pallas kernels, on_device(): pl.pallas_call(second_exchange, out_shape=MSG, in_specs=[VM], out_specs=V...  20.9 us
    pallas_call x1, Pallas kernels, on_device(): pl.pallas_call(functools.partial(conv_kernel, lats), out_shape=MSG, in_sp...  10.5 us
    unnamed x18, local copies, waits for them, and re-layouts  7.05 us
    pallas_call x1, Pallas kernels, on_device(): pl.pallas_call(mlp_kernel, out_shape=jax.ShapeDtypeStruct((NB, ROWS, C),...  2.62 us

commit v1 on v0

--- a/solution.py
+++ b/solution.py
@@ -189,34 +189,29 @@
 TN = (((0,), (0,)), ((), ()))
 
 
-def spread_rows(order_ref, own_ref, up_ref, down_ref, lat, lats, x_ref, d_ref, e_ref, f_ref):
+def rows_of(x_ref, r):
+    return x_ref[pl.ds(r, 64, stride=16), :].astype(BF)
+
+
+def twice(x):
+    return jnp.concatenate([x, x], axis=0)
+
+
+def turn_rows(order_ref, parts, first, last, rows, d_ref, e_ref):
+    eye = (iota((128, 128), 0) == iota((128, 128), 1)).astype(F32).astype(BF)
+    order = order_ref[...]
+    ex = lax.dot_general(eye, twice(last), NT, preferred_element_type=F32)
+    for i, r in enumerate(rows):
+        d_ref[first + i] = lax.dot_general(order, twice(parts[i]), NT, preferred_element_type=F32)
+        e_ref[first + i] = ex[8 * r : 8 * r + 8]
+
+
+def spread_rows(start, stop, d_ref, e_ref, f_ref):
     lane8 = iota((8, 128), 1)
     sub8 = iota((8, 128), 0)
     left = lane8 < 64
     both = (sub8 < 4) == left
     corner = (sub8 < 4) & left
-    eye = (iota((128, 128), 0) == iota((128, 128), 1)).astype(F32).astype(BF)
-    order = order_ref[...]
-
-    def load(which, rows, first, keep):
-        def rowsof(r):
-            x = x_ref[pl.ds(r, 64, stride=16), :]
-            if keep is not None:
-                x = jnp.where(keep, x, 0.0)
-            x = x.astype(BF)
-            return jnp.concatenate([x, x], axis=0)
-
-        x_ref[...] = which[...].reshape(1024, 128).astype(F32)
-        ex = lax.dot_general(eye, rowsof(15), NT, preferred_element_type=F32)
-        for i, r in enumerate(rows):
-            d_ref[first + i] = lax.dot_general(order, rowsof(r), NT, preferred_element_type=F32)
-            e_ref[first + i] = ex[8 * r : 8 * r + 8]
-
-    load(own_ref, range(ROWS), R, None)
-    load(up_ref, (13, 14), 0, lat > 0)
-    load(down_ref, (0, 1), ROWS + R, lat < lats - 1)
-    for step in range(9):
-        f_ref[step, pl.ds(304, 16), :] = jnp.zeros((16, 768), BF)
 
     def one(r, carry):
         at = pl.multiple_of(16 * r, 16)
@@ -237,7 +232,7 @@
                 f_ref[step, pl.ds(at, 16), pl.ds(128 * g, 128)] = jnp.concatenate([top, low], axis=0).astype(BF)
         return carry
 
-    lax.fori_loop(0, ROWS + 2 * R, one, 0)
+    lax.fori_loop(start, stop, one, 0)
 
 
 def convolve(t_ref, f_ref, w_ref, back_ref, final_ref, acc_ref, x_ref, z_ref, out_ref):
@@ -279,36 +274,12 @@
         out_ref[n] = result[16 * n : 16 * n + ROWS]
 
 
-def pack_kernel(f_ref, o_ref, roll_ref):
-    pack(f_ref, o_ref, roll_ref)
-
-
-def conv_kernel(lats, own_ref, up_ref, down_ref, sup_ref, sin_ref, filt_ref, order_ref, back_ref, final_ref, out_ref,
-                t_ref, w_ref, x_ref, d_ref, e_ref, f_ref, acc_ref, z_ref):
-    me = lax.axis_index("lon")
-    lat = lax.axis_index("lat")
-    build_weights(sup_ref, sin_ref, lat * ROWS, t_ref)
-    build_filter(filt_ref, me, w_ref)
-    spread_rows(order_ref, own_ref, up_ref, down_ref, lat, lats, x_ref, d_ref, e_ref, f_ref)
-    convolve(t_ref, f_ref, w_ref, back_ref, final_ref, acc_ref, x_ref, z_ref, out_ref)
-
-
-def mlp_kernel(m_ref, up_ref, down_ref, out_ref, turn_ref, c_ref):
-    unpack(m_ref, c_ref, turn_ref)
-    mlp(c_ref, up_ref, down_ref, out_ref)
-
-
-def greet(me, lat, lats, halo):
-    barrier = pltpu.get_barrier_semaphore()
-
-    def hail(i, carry):
+def hail(me, lat, lats, barrier):
+    def one(i, carry):
         pl.semaphore_signal(barrier, inc=1, device_id={"lon": lax.rem(me + i, OWN)}, device_id_type=MESH)
         return carry
 
-    lax.fori_loop(1, OWN, hail, 0)
-    if not halo:
-        pl.semaphore_wait(barrier, OWN - 1)
-        return
+    lax.fori_loop(1, OWN, one, 0)
 
     @pl.when(lat > 0)
     def _():
@@ -318,106 +289,144 @@
     def _():
         pl.semaphore_signal(barrier, inc=1, device_id={"lat": lat + 1}, device_id_type=MESH)
 
-    pl.semaphore_wait(barrier, OWN - 1 + (lat > 0).astype(jnp.int32) + (lat < lats - 1).astype(jnp.int32))
-
-
-def exchange(me, src, dst, send_sem, recv_sem, copy_sem):
-    def send(i, carry):
-        p = lax.rem(me + i, OWN)
+
+def send_all(me, src, dst, send_sem, recv_sem):
+    across, along, up = me // 16, me // 8 % 2, me % 8
+
+    def send(i, side):
+        p = lax.rem(across + i // 8, 4) * 16 + side * 8 + lax.rem(up + i % 8, 8)
         pltpu.make_async_remote_copy(
             src.at[p], dst.at[me], send_sem, recv_sem, device_id={"lon": p}, device_id_type=MESH
         ).start()
-        return carry
-
-    lax.fori_loop(1, OWN, send, 0)
-    mine = pltpu.make_async_copy(src.at[me], dst.at[me], copy_sem)
-    mine.start()
-    mine.wait()
-    every = pltpu.make_async_remote_copy(
+
+    def far(i, carry):
+        send(i, 1 - along)
+        return carry
+
+    def near(i, carry):
+        send(i, along)
+        return carry
+
+    lax.fori_loop(0, 32, far, 0)
+    lax.fori_loop(1, 32, near, 0)
+
+
+def all_sent(me, src, dst, send_sem, recv_sem):
+    return pltpu.make_async_remote_copy(
         src.at[pl.ds(0, OWN - 1)], dst.at[pl.ds(0, OWN - 1)], send_sem, recv_sem,
         device_id={"lon": lax.rem(me + 1, OWN)}, device_id_type=MESH,
     )
-    every.wait_recv()
-    every.wait_send()
-
-
-def first_exchange(lats, src, own, up, down, send_sem, recv_sem, copy_sem, halo_send, halo_recv):
+
+
+def kernel(lats, pts_hbm, sup_ref, sin_ref, filt_ref, order_ref, back_ref, final_ref, wup_hbm, wdown_hbm, out_ref,
+           pts, wup, wdown, roll_ref, msg, own, halo_out, halo_in, t_ref, w_ref, x_ref, d_ref, e_ref, f_ref, acc_ref,
+           z_ref, back, pieces, turn_ref, c_ref, load_sem, send_sem, recv_sem, halo_send, halo_recv):
     me = lax.axis_index("lon")
     lat = lax.axis_index("lat")
-    greet(me, lat, lats, True)
-    exchange(me, src, own, send_sem, recv_sem, copy_sem)
-
-    def halo(to, dst, i):
+    barrier = pltpu.get_barrier_semaphore()
+    fetch = pltpu.make_async_copy(pts_hbm, pts, load_sem.at[0])
+    fetch.start()
+    hail(me, lat, lats, barrier)
+    fetch_up = pltpu.make_async_copy(wup_hbm, wup, load_sem.at[1])
+    fetch_down = pltpu.make_async_copy(wdown_hbm, wdown, load_sem.at[2])
+    fetch_up.start()
+    fetch_down.start()
+    fetch.wait()
+    pack(pts, msg, roll_ref)
+    pl.semaphore_wait(barrier, OWN - 1 + (lat > 0).astype(jnp.int32) + (lat < lats - 1).astype(jnp.int32))
+    send_all(me, msg, own, send_sem.at[0], recv_sem.at[0])
+    own[me] = msg[me]
+    build_weights(sup_ref, sin_ref, lat * ROWS, t_ref)
+    build_filter(filt_ref, me, w_ref)
+    for step in range(9):
+        f_ref[step, pl.ds(304, 16), :] = jnp.zeros((16, 768), BF)
+    first = all_sent(me, msg, own, send_sem.at[0], recv_sem.at[0])
+    first.wait_recv()
+
+    def halo(to, i):
         return pltpu.make_async_remote_copy(
-            own, dst, halo_send.at[i], halo_recv.at[i], device_id={"lat": to}, device_id_type=MESH
+            halo_out.at[i], halo_in.at[i], halo_send.at[i], halo_recv.at[i], device_id={"lat": to}, device_id_type=MESH
         )
 
+    x_ref[...] = own[...].reshape(1024, 128).astype(F32)
+    last = rows_of(x_ref, 15)
+    for i, rows in enumerate(((0, 1), (13, 14))):
+        for j, r in enumerate(rows):
+            halo_out[i, j] = rows_of(x_ref, r)
+        halo_out[i, 2] = last
+
     @pl.when(lat > 0)
     def _():
-        halo(lat - 1, down, 0).start()
+        halo(lat - 1, 0).start()
 
     @pl.when(lat < lats - 1)
     def _():
-        halo(lat + 1, up, 1).start()
+        halo(lat + 1, 1).start()
+
+    turn_rows(order_ref, [rows_of(x_ref, r) for r in range(ROWS)], R, last, range(ROWS), d_ref, e_ref)
+    spread_rows(R, ROWS + R, d_ref, e_ref, f_ref)
 
     @pl.when(lat > 0)
     def _():
-        halo(lat - 1, down, 0).wait_send()
-        halo(lat - 1, up, 1).wait_recv()
+        halo(lat - 1, 0).wait_send()
+        halo(lat - 1, 1).wait_recv()
+
+    @pl.when(lat == 0)
+    def _():
+        halo_in[1] = jnp.zeros((3, OWN, 128), BF)
 
     @pl.when(lat < lats - 1)
     def _():
-        halo(lat + 1, up, 1).wait_send()
-        halo(lat + 1, down, 0).wait_recv()
-
-
-def second_exchange(src, own, send_sem, recv_sem, copy_sem):
-    me = lax.axis_index("lon")
-    greet(me, None, None, False)
-    exchange(me, src, own, send_sem, recv_sem, copy_sem)
+        halo(lat + 1, 1).wait_send()
+        halo(lat + 1, 0).wait_recv()
+
+    @pl.when(lat == lats - 1)
+    def _():
+        halo_in[0] = jnp.zeros((3, OWN, 128), BF)
+
+    turn_rows(order_ref, [halo_in[1, 0], halo_in[1, 1]], 0, halo_in[1, 2], (13, 14), d_ref, e_ref)
+    turn_rows(order_ref, [halo_in[0, 0], halo_in[0, 1]], ROWS + R, halo_in[0, 2], (0, 1), d_ref, e_ref)
+    spread_rows(0, R, d_ref, e_ref, f_ref)
+    spread_rows(ROWS + R, ROWS + 2 * R, d_ref, e_ref, f_ref)
+    convolve(t_ref, f_ref, w_ref, back_ref, final_ref, acc_ref, x_ref, z_ref, back)
+    send_all(me, back, pieces, send_sem.at[1], recv_sem.at[1])
+    pieces[me] = back[me]
+    fetch_up.wait()
+    fetch_down.wait()
+    first.wait_send()
+    second = all_sent(me, back, pieces, send_sem.at[1], recv_sem.at[1])
+    second.wait_recv()
+    unpack(pieces, c_ref, turn_ref)
+    mlp(c_ref, wup, wdown, out_ref)
+    second.wait_send()
 
 
 VM = pl.BlockSpec(memory_space=pltpu.VMEM)
 SM = pl.BlockSpec(memory_space=pltpu.SMEM)
-MSG = jax.ShapeDtypeStruct((OWN, 16, 128), BF)
-
-
-def params(**kw):
-    return pltpu.CompilerParams(vmem_limit_bytes=48 << 20, **kw)
+ANY = pl.BlockSpec(memory_space=pl.ANY)
 
 
 def on_device(lats, fields, support, filter_weight, w_up, w_down):
     points = jnp.transpose(fields, (2, 0, 1))
-    messages = pl.pallas_call(
-        pack_kernel, out_shape=MSG, in_specs=[VM], out_specs=VM,
-        scratch_shapes=[pltpu.VMEM((NB, 16, 768), F32)], compiler_params=params(), name="pack",
-    )(points)
     dma = pltpu.SemaphoreType.DMA
-    own, up, down = pl.pallas_call(
-        functools.partial(first_exchange, lats), out_shape=(MSG,) * 3, in_specs=[VM], out_specs=(VM,) * 3,
-        scratch_shapes=[dma, dma, dma, dma((2,)), dma((2,))],
-        compiler_params=params(collective_id=0, has_side_effects=True), name="to_owners",
-    )(messages)
-    back = pl.pallas_call(
-        functools.partial(conv_kernel, lats), out_shape=MSG,
-        in_specs=[VM, VM, VM, SM, SM, VM, VM, VM, VM], out_specs=VM,
+    result = pl.pallas_call(
+        functools.partial(kernel, lats), out_shape=jax.ShapeDtypeStruct((NB, ROWS, C), BF),
+        in_specs=[ANY, SM, SM, VM, VM, VM, VM, ANY, ANY], out_specs=VM,
         scratch_shapes=[
+            pltpu.VMEM((NB, ROWS, C), BF), pltpu.VMEM(w_up.shape, BF), pltpu.VMEM(w_up.shape, BF),
+            pltpu.VMEM((NB, 16, 768), F32), pltpu.VMEM((OWN, 16, 128), BF), pltpu.VMEM((OWN, 16, 128), BF),
+            pltpu.VMEM((2, 3, OWN, 128), BF), pltpu.VMEM((2, 3, OWN, 128), BF),
             pltpu.VMEM((4, 256, 1152), BF), pltpu.VMEM((K, 768), F32), pltpu.VMEM((1024, 128), F32),
             pltpu.VMEM((ROWS + 2 * R, 128, 128), F32), pltpu.VMEM((ROWS + 2 * R, 8, 128), F32),
             pltpu.VMEM((9, 320, 768), BF), pltpu.VMEM((256, 768), F32), pltpu.VMEM((256, 128), BF),
+            pltpu.VMEM((OWN, 16, 128), BF), pltpu.VMEM((OWN, 16, 128), BF),
+            pltpu.VMEM((OWN, 16, 128), F32), pltpu.VMEM((192, 768), F32),
+            dma((3,)), dma((2,)), dma((2,)), dma((2,)), dma((2,)),
         ],
-        compiler_params=params(), name="convolve",
-    )(own, up, down, support.T, jnp.asarray(sines()), filter_weight.T, jnp.asarray(order_matrix(), BF),
-      jnp.asarray(back_matrix(), BF), jnp.asarray(last_matrix(), BF))
-    pieces = pl.pallas_call(
-        second_exchange, out_shape=MSG, in_specs=[VM], out_specs=VM, scratch_shapes=[dma, dma, dma],
-        compiler_params=params(collective_id=1, has_side_effects=True), name="to_longitudes",
-    )(back)
-    result = pl.pallas_call(
-        mlp_kernel, out_shape=jax.ShapeDtypeStruct((NB, ROWS, C), BF), in_specs=[VM] * 3, out_specs=VM,
-        scratch_shapes=[pltpu.VMEM((OWN, 16, 128), F32), pltpu.VMEM((192, 768), F32)],
-        compiler_params=params(), name="channels",
-    )(pieces, w_up, w_down.T)
+        compiler_params=pltpu.CompilerParams(vmem_limit_bytes=60 << 20, collective_id=0, has_side_effects=True),
+        name="block",
+    )(points, support.T, jnp.asarray(sines()), filter_weight.T, jnp.asarray(order_matrix(), BF),
+      jnp.asarray(back_matrix(), BF), jnp.asarray(last_matrix(), BF), w_up, w_down.T)
     return jnp.transpose(result, (1, 2, 0))
 
 

time: 80.4 us -> 66.2 us (0.82)
  Pallas kernels: 72.8 us -> 64.3 us
  local copies, waits for them, and re-layouts: 7.05 us -> 1.69 us
    pallas_call x5 -> x1, Pallas kernels: 72.8 us -> 64.3 us  [on_device(): pl.pallas_call(functools.partial(kernel, lats), out_shape=jax.ShapeDtypeS...]
    unnamed x18 -> x1, local copies, waits for them, and re-layouts: 7.05 us -> 1.69 us
where the time goes in v1:
time: 66.2 us; the launch traced here: 66 us
  Pallas kernels  64.3 us (97%)
  local copies, waits for them, and re-layouts  1.69 us (3%)
    pallas_call x1, Pallas kernels, on_device(): pl.pallas_call(functools.partial(kernel, lats), out_shape=jax.ShapeDtypeS...  64.3 us
    unnamed x1, local copies, waits for them, and re-layouts  1.69 us

profile of v1, /device:TPU:1, one launch (start us, length us, event | category | flops | bytes accessed | tf_op | source)
XLA Modules:
  0.0 66.0 jit_solution(5955370572257830292)
XLA Ops:
  0.0 64.3 %block.1 = bf16[12,15,641]{2,1,0:T(8,128)(2,1)} custom-call(bf16[12,15,641]{2,1,0:T(8,128)(2,1)} %bitcast.7, s32[5,180]{1,0:T(8,128)} %bitcast.8, f32[1,192]{1,0:T(1,128)} %constant.8.clone.sin_ref, bf16[4,641]{1,0:T(4,128)(2,1)} %bitcast.9, bf16[128,128]{1,0:T(8,128)(2,1)} %constant.9.clone.order_ref, bf16[96,256]{1,0:T(8,128)(2,1)} %constant.10.clone.back_ref, ...), custom_call_target="tpu_custom_call" | custom-call | tf_op jit(solution)/shard_map/block/pallas_call | solution.py:412
  64.3 1.7 %copy.11 = bf16[15,641,12]{1,0,2:T(8,128)(2,1)} copy(bf16[15,641,12]{1,0,2:T(8,128)(2,1)} %bitcast.6) | data formatting | bytes 461520

commit v2 on v1

v2 whole, which is shorter than its diff:
```python
import functools
import math

import jax
import jax.numpy as jnp
import numpy as np
from jax import lax
from jax.experimental import pallas as pl
from jax.experimental.pallas import tpu as pltpu
from jax.sharding import PartitionSpec as P

MESH = pl.DeviceIdType.MESH
NB = 12
ROWS = 15
C = 641
CH = 10
OWN = 64
K = 4
R = 2
F32 = jnp.float32
BF = jnp.bfloat16


def iota(shape, dim):
    return lax.broadcasted_iota(jnp.int32, shape, dim)


HALF = 5


def prepare(f_ref, roll_ref, last_ref):
    lane = iota((16, 128), 1)
    sub = iota((16, 128), 0)
    lane8 = iota((8, 128), 1)
    spread = jnp.zeros((16, 128), F32)
    extras = [jnp.zeros((16, 128), F32), jnp.zeros((16, 128), F32)]
    for n in range(NB):
        x = f_ref[n].astype(F32)
        x = jnp.concatenate([x, jnp.zeros((ROWS, 768 - C), F32)], axis=1)
        x = jnp.concatenate([x, jnp.zeros((1, 768), F32)], axis=0)
        roll_ref[n] = pltpu.roll(x, HALF * n, 1) if n else x
        col = jnp.broadcast_to(x[:, 640:641], (16, 128))
        if n < 8:
            extras[n // 4] = jnp.where(lane % 64 == 60 + n % 4, col, extras[n // 4])
        else:
            spread = jnp.where(lane == 64 + 4 * sub + (n - 8), col, spread)
    row = jnp.sum(jnp.where(sub < ROWS, spread, 0.0), axis=0, keepdims=True)
    for h in range(2):
        last_ref[h] = jnp.where(lane8 < 64, extras[h][:8], extras[h][8:])
    last_ref[2] = jnp.broadcast_to(row, (8, 128))


def pack(h, roll_ref, last_ref, o_ref):
    lane = iota((8, 128), 1)
    sub = iota((8, 128), 0)
    for p in range(OWN):
        begin = CH * p + HALF * h
        cut = begin % 128
        here = (lane - cut) & 127
        acc = [None, None]
        for n in range(NB):
            lo = begin + HALF * n
            first, final = lo // 128, (lo + HALF - 1) // 128
            for i in range(2):
                x = roll_ref[n, pl.ds(8 * i, 8), pl.ds(first * 128, 128)]
                if first != final:
                    x = jnp.where(lane >= 64, x, roll_ref[n, pl.ds(8 * i, 8), pl.ds(final * 128, 128)])
                acc[i] = x if n == 0 else jnp.where(here >= HALF * n, x, acc[i])
        low = pltpu.roll(acc[0], 128 - cut, 1) if cut else acc[0]
        high = pltpu.roll(acc[1], (192 - cut) % 128, 1) if cut != 64 else acc[1]
        x = jnp.where(lane < 64, low, high)
        x = jnp.where((lane & 63) >= 60, last_ref[h], x)
        if h:
            x = jnp.where((sub == 7) & (lane >= 64) & (lane < 124), last_ref[2], x)
        o_ref[h, p] = x.astype(BF)


def turn_pieces(h, m_ref, turn_ref):
    for q in range(OWN):
        x = m_ref[h, q].astype(F32)
        cut = (CH * q + HALF * h) % 128
        turn_ref[2 * q + h, pl.ds(0, 8), :] = pltpu.roll(x, cut, 1) if cut else x
        turn_ref[2 * q + h, pl.ds(8, 8), :] = pltpu.roll(x, (cut + 64) % 128, 1) if cut != 64 else x


def unpack(turn_ref, last, c_ref):
    lane = iota((16, 128), 1)
    for n in range(NB):
        tiles = []
        for t in range(6):
            acc = jnp.zeros((16, 128), F32)
            for i in range(2 * OWN):
                a = HALF * (i + n) - t * 128
                if -HALF < a < 128:
                    acc = turn_ref[i] if a <= 0 else jnp.where(lane >= a, turn_ref[i], acc)
            tiles.append(acc)
        full = jnp.concatenate(tiles, axis=1)
        if n:
            full = pltpu.roll(full, 768 - HALF * n, 1)
        c_ref[pl.ds(16 * n, 16), pl.ds(0, 640)] = full[:, :640]
        c_ref[pl.ds(16 * n, 16), pl.ds(640, 128)] = jnp.where(lane == 0, last[:, n : n + 1], 0.0)


def order_matrix():
    out = np.zeros((2, 2, 64, 128), np.float32)
    for h in range(2):
        for half in range(2):
            base = 64 * half
            for g in range(2):
                for n in range(NB):
                    for c in range(2):
                        j = 24 * g + (8 * c + n if n < 8 else 16 + 4 * c + n - 8)
                        out[h, half, j, base + HALF * n + 2 * g + c] = 1
            for n in range(NB):
                j = 48 + n if n < 8 or h else 48 + n + 4
                out[h, half, j, base + HALF * n + 4] = 1
            for t in range(4):
                out[h, half, 60 + t if h else 56 + t, base + 60 + t] = 1
    return out


def row_matrix():
    out = np.zeros((128, 128), np.float32)
    for r in range(ROWS):
        for t in range(4):
            out[8 * r + t, 64 + 4 * r + t] = 1
    return out


def back_matrix():
    out = np.zeros((2, 2, 48, 384), np.float32)
    for h in range(2):
        for half in range(2):
            base = 64 * half
            for n in range(NB):
                for g in range(2):
                    out[h, half, 16 * g + n, base + HALF * n + 2 * g] = 1
                    out[h, half, 16 * g + (n if n < 8 else n + 4), 128 + base + HALF * n + 2 * g + 1] = 1
                out[h, half, 32 + (n if n < 8 or h else n + 4), base + HALF * n + 4] = 1
                out[h, half, 32 + n, 256 + n] = 1
    return out


def sines():
    i = np.arange(192, dtype=np.float64) - R
    return np.sin(np.pi * (i + 0.5) / 180.0).astype(np.float32)[None]


def build_weights(sup_ref, sin_ref, start, t_ref):
    lane = iota((16, 128), 1)
    rlane = lane // 16
    s = lane % 16
    n_in = jnp.where(s < 12, s, s - 4)
    sub = iota((16, 128), 0)
    n_out = jnp.where(sub < 12, sub, sub - 4)
    diff = (n_in - n_out).astype(F32)

    def one(o, carry):
        local = o % 4
        group = o // 4
        row = jnp.minimum(start + o, 179)
        d = rlane - local
        width = jnp.ones((16, 128), F32)
        sine = jnp.zeros((16, 128), F32)
        for j in range(2 * R + 1):
            width = jnp.where(d == j, sup_ref[j, row].astype(F32), width)
            sine = jnp.where(d == j, sin_ref[0, row + j], sine)
        ok = (d >= 0) & (d <= 2 * R)
        scale = jnp.where(ok, sine / jnp.sqrt((2.0 * R + 1.0) * (2.0 * width + 1.0)), 0.0)
        lat = (d - R).astype(F32) / (R + 1.0)
        lat2 = lat * lat
        base = pl.multiple_of(local * 64, 64)
        for step in range(9):
            m = diff + float(12 * (step - 4))
            lon = m / (width + 1.0)
            radius = jnp.sqrt(lat2 + lon * lon) * (K - 1.0)
            w = jnp.where(jnp.abs(m) <= width, scale, 0.0)
            for k in range(K):
                hat = jnp.maximum(0.0, 1.0 - jnp.abs(radius - float(k)))
                t_ref[group, pl.ds(base + 16 * k, 16), pl.ds(128 * step, 128)] = (hat * w).astype(BF)
        return carry

    lax.fori_loop(0, 16, one, 0)


def build_filter(filt_ref, me, w_ref):
    lane = iota((C, 768), 1)
    slot = lane // 64 % 6
    chan = me * CH + HALF * (lane // 384) + slot
    want = jnp.where(slot == 5, C - 1, chan)
    pick = jnp.where(iota((C, 768), 0) == want, 1.0, 0.0).astype(BF)
    w_ref[...] = jnp.dot(filt_ref[...], pick, preferred_element_type=F32)


NT = (((1,), (1,)), ((), ()))
TN = (((0,), (0,)), ((), ()))


def rows_of(x_ref, r):
    return x_ref[pl.ds(r % 8, 64, stride=8), :].astype(BF)


def twice(x):
    return jnp.concatenate([x, x], axis=0)


def turn_rows(h, order_ref, row_ref, parts, last, first, rows, d_ref, e_ref, z_ref):
    if h:
        ex = lax.dot_general(row_ref[...], twice(last), NT, preferred_element_type=F32)
    for i, r in enumerate(rows):
        turned = lax.dot_general(order_ref[h, r // 8], twice(parts[i]), NT, preferred_element_type=F32)
        d_ref[first + i] = turned
        if h:
            e_ref[first + i] = ex[8 * r : 8 * r + 8]
        else:
            z_ref[first + i] = turned[56:64]


def spread_rows(h, start, stop, d_ref, e_ref, z_ref, f_ref):
    lane8 = iota((8, 128), 1)
    sub8 = iota((8, 128), 0)
    left = lane8 < 64
    upper = sub8 < 4
    both = upper == left

    def one(r, carry):
        at = pl.multiple_of(16 * r, 16)
        for step in range(9):
            shift = (4 - step) % 128

            def roll(x):
                return pltpu.roll(x, shift, 1) if shift else x

            turned = roll(d_ref[r])
            for g in range(3):
                if g < 2:
                    top = jnp.where(left, turned[24 * g : 24 * g + 8], turned[24 * g + 8 : 24 * g + 16])
                    low = jnp.where(both, turned[24 * g + 16 : 24 * g + 24], 0.0)
                elif h:
                    tail = turned[56:64]
                    top = jnp.where(left, turned[48:56], jnp.where(upper, roll(z_ref[r]), tail))
                    low = jnp.where(upper, jnp.where(left, tail, roll(e_ref[r])), 0.0)
                else:
                    top = jnp.where(left, turned[48:56], 0.0)
                    low = jnp.where(left & (sub8 >= 4), turned[56:64], 0.0)
                f_ref[step, pl.ds(at, 16), pl.ds(128 * g, 128)] = jnp.concatenate([top, low], axis=0).astype(BF)
        return carry

    lax.fori_loop(start, stop, one, 0)


def convolve(h, groups, t_ref, f_ref, w_ref, back_ref, acc_ref, x_ref, ex_ref):
    for g in groups:
        at = 64 * g
        rhs = jnp.concatenate([f_ref[step, pl.ds(at, 128), :] for step in range(9)], axis=0)
        acc_ref[...] = jnp.dot(t_ref[g], rhs, preferred_element_type=F32)
        for o in range(4):
            conv = jnp.zeros((16, 384), F32)
            for k in range(K):
                conv = conv + acc_ref[pl.ds(64 * o + 16 * k, 16), :] * w_ref[pl.ds(k, 1), pl.ds(384 * h, 384)]
            centre = f_ref[4, pl.ds(at + 16 * (o + R), 16), :].astype(F32)
            comb = (centre + conv).astype(BF)
            stack = jnp.concatenate([comb[:, 128 * i : 128 * i + 128] for i in range(3)], axis=0)
            moved = lax.dot_general(stack, back_ref[h, g // 2], TN, preferred_element_type=F32)
            value = moved[:64, :128] + moved[64:, 128:256]
            row = (4 * g + o) % 8
            if g in (0, 3):
                value = value + x_ref[pl.ds(row, 64, stride=8), :]
            x_ref[pl.ds(row, 64, stride=8), :] = value
            if h:
                ex_ref[4 * g + o] = moved[64:, 256:]


def mlp(c_ref, up_ref, down_ref, out_ref):
    lane = iota((192, 768), 1)
    values = c_ref[...]
    mean = jnp.sum(values, axis=1, keepdims=True) * (1.0 / C)
    centered = jnp.where(lane < C, values - mean, 0.0)
    spread = jnp.sum(centered * centered, axis=1, keepdims=True) * (1.0 / C)
    normed = (centered * lax.rsqrt(spread + 1e-05)).astype(BF)[:, :C]
    raised = jnp.dot(normed, up_ref[...], preferred_element_type=F32)
    hidden = (0.5 * raised * (1.0 + lax.erf(raised * math.sqrt(0.5)))).astype(BF)
    lowered = lax.dot_general(hidden, down_ref[...], NT, preferred_element_type=F32)
    result = (values[:, :C] + lowered).astype(BF)
    for n in range(NB):
        out_ref[n] = result[16 * n : 16 * n + ROWS]


def hail(me, lat, lats, barrier):
    def one(i, carry):
        pl.semaphore_signal(barrier, inc=1, device_id={"lon": lax.rem(me + i, OWN)}, device_id_type=MESH)
        return carry

    lax.fori_loop(1, OWN, one, 0)

    @pl.when(lat > 0)
    def _():
        pl.semaphore_signal(barrier, inc=1, device_id={"lat": lat - 1}, device_id_type=MESH)

    @pl.when(lat < lats - 1)
    def _():
        pl.semaphore_signal(barrier, inc=1, device_id={"lat": lat + 1}, device_id_type=MESH)


def send_all(me, src, dst, send_sem, recv_sem):
    across, along, up = me // 16, me // 8 % 2, me % 8

    def send(i, side):
        p = lax.rem(across + i // 8, 4) * 16 + side * 8 + lax.rem(up + i % 8, 8)
        pltpu.make_async_remote_copy(
            src.at[p], dst.at[me], send_sem, recv_sem, device_id={"lon": p}, device_id_type=MESH
        ).start()

    def far(i, carry):
        send(i, 1 - along)
        return carry

    def near(i, carry):
        send(i, along)
        return carry

    lax.fori_loop(0, 32, far, 0)
    lax.fori_loop(1, 32, near, 0)


def all_sent(me, src, dst, send_sem, recv_sem):
    return pltpu.make_async_remote_copy(
        src.at[pl.ds(0, OWN - 1)], dst.at[pl.ds(0, OWN - 1)], send_sem, recv_sem,
        device_id={"lon": lax.rem(me + 1, OWN)}, device_id_type=MESH,
    )


def kernel(lats, pts_hbm, sup_ref, sin_ref, filt_ref, order_ref, row_ref, back_ref, wup_hbm, wdown_hbm, out_ref,
           pts, wup, wdown, roll_ref, last_ref, msg, own, halo_out, halo_in, t_ref, w_ref, x_ref, d_ref, e_ref, z_ref,
           f_ref, acc_ref, ex_ref, back, pieces, turn_ref, c_ref, load_sem, send_sem, recv_sem, halo_send, halo_recv):
    me = lax.axis_index("lon")
    lat = lax.axis_index("lat")
    barrier = pltpu.get_barrier_semaphore()
    fetch = pltpu.make_async_copy(pts_hbm, pts, load_sem.at[0])
    fetch.start()
    hail(me, lat, lats, barrier)
    fetch_up = pltpu.make_async_copy(wup_hbm, wup, load_sem.at[1])
    fetch_down = pltpu.make_async_copy(wdown_hbm, wdown, load_sem.at[2])
    fetch_up.start()
    fetch_down.start()
    fetch.wait()
    prepare(pts, roll_ref, last_ref)
    pack(0, roll_ref, last_ref, msg)
    pl.semaphore_wait(barrier, OWN - 1 + (lat > 0).astype(jnp.int32) + (lat < lats - 1).astype(jnp.int32))
    send_all(me, msg.at[0], own.at[0], send_sem.at[0], recv_sem.at[0])
    pack(1, roll_ref, last_ref, msg)
    send_all(me, msg.at[1], own.at[1], send_sem.at[1], recv_sem.at[1])
    for h in range(2):
        own[h, me] = msg[h, me]
    build_weights(sup_ref, sin_ref, lat * ROWS, t_ref)
    build_filter(filt_ref, me, w_ref)
    for step in range(9):
        f_ref[step, pl.ds(304, 16), :] = jnp.zeros((16, 384), BF)

    def halo(h, to, i):
        return pltpu.make_async_remote_copy(
            halo_out.at[h, i], halo_in.at[h, i], halo_send.at[h, i], halo_recv.at[h, i],
            device_id={"lat": to}, device_id_type=MESH,
        )

    for h in range(2):
        all_sent(me, msg.at[h], own.at[h], send_sem.at[h], recv_sem.at[h]).wait_recv()
        x_ref[...] = own[h].reshape(512, 128).astype(F32)
        for i, rows in enumerate(((0, 1), (13, 14))):
            for j, r in enumerate(rows):
                halo_out[h, i, j] = rows_of(x_ref, r)
            halo_out[h, i, 2] = rows_of(x_ref, 15)

        @pl.when(lat > 0)
        def _():
            halo(h, lat - 1, 0).start()

        @pl.when(lat < lats - 1)
        def _():
            halo(h, lat + 1, 1).start()

        turn_rows(h, order_ref, row_ref, [rows_of(x_ref, r) for r in range(ROWS)], rows_of(x_ref, 15), R, range(ROWS),
                  d_ref, e_ref, z_ref)
        spread_rows(h, R, ROWS + R, d_ref, e_ref, z_ref, f_ref)
        convolve(h, (1, 2), t_ref, f_ref, w_ref, back_ref, acc_ref, x_ref, ex_ref)

        @pl.when(lat > 0)
        def _():
            halo(h, lat - 1, 1).wait_recv()

        @pl.when(lat == 0)
        def _():
            halo_in[h, 1] = jnp.zeros((3, OWN, 128), BF)

        @pl.when(lat < lats - 1)
        def _():
            halo(h, lat + 1, 0).wait_recv()

        @pl.when(lat == lats - 1)
        def _():
            halo_in[h, 0] = jnp.zeros((3, OWN, 128), BF)

        turn_rows(h, order_ref, row_ref, [halo_in[h, 1, 0], halo_in[h, 1, 1]], halo_in[h, 1, 2], 0, (13, 14),
                  d_ref, e_ref, z_ref)
        turn_rows(h, order_ref, row_ref, [halo_in[h, 0, 0], halo_in[h, 0, 1]], halo_in[h, 0, 2], ROWS + R, (0, 1),
                  d_ref, e_ref, z_ref)
        spread_rows(h, 0, R, d_ref, e_ref, z_ref, f_ref)
        spread_rows(h, ROWS + R, ROWS + 2 * R, d_ref, e_ref, z_ref, f_ref)
        convolve(h, (0, 3), t_ref, f_ref, w_ref, back_ref, acc_ref, x_ref, ex_ref)
        back[h] = x_ref[...].reshape(64, 8, 128).astype(BF)
        send_all(me, back.at[h], pieces.at[h], send_sem.at[2 + h], recv_sem.at[2 + h])
        pieces[h, me] = back[h, me]
    fetch_up.wait()
    fetch_down.wait()
    for h in range(2):
        all_sent(me, msg.at[h], own.at[h], send_sem.at[h], recv_sem.at[h]).wait_send()

        @pl.when(lat > 0)
        def _():
            halo(h, lat - 1, 0).wait_send()

        @pl.when(lat < lats - 1)
        def _():
            halo(h, lat + 1, 1).wait_send()

    last = jnp.concatenate([ex_ref[o, pl.ds(me, 1), :] for o in range(16)], axis=0)
    for h in range(2):
        all_sent(me, back.at[h], pieces.at[h], send_sem.at[2 + h], recv_sem.at[2 + h]).wait_recv()
        turn_pieces(h, pieces, turn_ref)
    unpack(turn_ref, last, c_ref)
    mlp(c_ref, wup, wdown, out_ref)
    for h in range(2):
        all_sent(me, back.at[h], pieces.at[h], send_sem.at[2 + h], recv_sem.at[2 + h]).wait_send()


VM = pl.BlockSpec(memory_space=pltpu.VMEM)
SM = pl.BlockSpec(memory_space=pltpu.SMEM)
ANY = pl.BlockSpec(memory_space=pl.ANY)


def on_device(lats, fields, support, filter_weight, w_up, w_down):
    points = jnp.transpose(fields, (2, 0, 1))
    dma = pltpu.SemaphoreType.DMA
    result = pl.pallas_call(
        functools.partial(kernel, lats), out_shape=jax.ShapeDtypeStruct((NB, ROWS, C), BF),
        in_specs=[ANY, SM, SM, VM, VM, VM, VM, ANY, ANY], out_specs=VM,
        scratch_shapes=[
            pltpu.VMEM((NB, ROWS, C), BF), pltpu.VMEM(w_up.shape, BF), pltpu.VMEM(w_up.shape, BF),
            pltpu.VMEM((NB, 16, 768), F32), pltpu.VMEM((3, 8, 128), F32),
            pltpu.VMEM((2, OWN, 8, 128), BF), pltpu.VMEM((2, OWN, 8, 128), BF),
            pltpu.VMEM((2, 2, 3, OWN, 128), BF), pltpu.VMEM((2, 2, 3, OWN, 128), BF),
            pltpu.VMEM((4, 256, 1152), BF), pltpu.VMEM((K, 768), F32), pltpu.VMEM((512, 128), F32),
            pltpu.VMEM((ROWS + 2 * R, 64, 128), F32), pltpu.VMEM((ROWS + 2 * R, 8, 128), F32),
            pltpu.VMEM((ROWS + 2 * R, 8, 128), F32),
            pltpu.VMEM((9, 320, 384), BF), pltpu.VMEM((256, 384), F32), pltpu.VMEM((16, OWN, 128), F32),
            pltpu.VMEM((2, OWN, 8, 128), BF), pltpu.VMEM((2, OWN, 8, 128), BF),
            pltpu.VMEM((2 * OWN, 16, 128), F32), pltpu.VMEM((192, 768), F32),
            dma((3,)), dma((4,)), dma((4,)), dma((2, 2)), dma((2, 2)),
        ],
        compiler_params=pltpu.CompilerParams(vmem_limit_bytes=60 << 20, collective_id=0, has_side_effects=True),
        name="block",
    )(points, support.T, jnp.asarray(sines()), filter_weight.T, jnp.asarray(order_matrix(), BF),
      jnp.asarray(row_matrix(), BF), jnp.asarray(back_matrix(), BF), w_up, w_down.T)
    return jnp.transpose(result, (1, 2, 0))


def solution(mesh):
    in_specs = (P("lat", None, "lon"), P(), P(), P(), P())
    out_specs = P("lat", None, "lon")
    return jax.shard_map(
        functools.partial(on_device, mesh.shape["lat"]), mesh=mesh, in_specs=in_specs, out_specs=out_specs,
        check_vma=False,
    )
```

time: 66.2 us -> 64.3 us (0.971)
  the two profiles are of different devices: /device:TPU:1 before, /device:TPU:193 now
where the time goes in v2:
time: 64.3 us; the launch traced here: 64.1 us
  Pallas kernels  62.4 us (97%)
  local copies, waits for them, and re-layouts  1.69 us (3%)
    pallas_call x1, Pallas kernels, on_device(): pl.pallas_call(functools.partial(kernel, lats), out_shape=jax.ShapeDtypeS...  62.4 us
    unnamed x1, local copies, waits for them, and re-layouts  1.69 us

profile of v2, /device:TPU:193, one launch (start us, length us, event | category | flops | bytes accessed | tf_op | source)
XLA Modules:
  0.0 64.1 jit_solution(4942131829793563004)
XLA Ops:
  0.0 62.4 %block.1 = bf16[12,15,641]{2,1,0:T(8,128)(2,1)} custom-call(bf16[12,15,641]{2,1,0:T(8,128)(2,1)} %bitcast.7, s32[5,180]{1,0:T(8,128)} %bitcast.8, f32[1,192]{1,0:T(1,128)} %constant.8.clone.sin_ref, bf16[4,641]{1,0:T(4,128)(2,1)} %bitcast.9, bf16[2,2,64,128]{3,2,1,0:T(8,128)(2,1)} %constant.9.clone.order_ref, bf16[128,128]{1,0:T(8,128)(2,1)} %constant.10.clone.row_ref, ...), custom_call_target="tpu_custom_call" | custom-call | tf_op jit(solution)/shard_map/block/pallas_call | solution.py:444
  62.4 1.7 %copy.11 = bf16[15,641,12]{1,0,2:T(8,128)(2,1)} copy(bf16[15,641,12]{1,0,2:T(8,128)(2,1)} %bitcast.6) | data formatting | bytes 461520

commit v3 on v2

--- a/solution.py
+++ b/solution.py
@@ -330,8 +330,8 @@
     )
 
 
-def kernel(lats, pts_hbm, sup_ref, sin_ref, filt_ref, order_ref, row_ref, back_ref, wup_hbm, wdown_hbm, out_ref,
-           pts, wup, wdown, roll_ref, last_ref, msg, own, halo_out, halo_in, t_ref, w_ref, x_ref, d_ref, e_ref, z_ref,
+def kernel(lats, pts_hbm, sup_hbm, sin_hbm, filt_hbm, order_hbm, row_hbm, back_hbm, wup_hbm, wdown_hbm, out_ref,
+           sup_ref, sin_ref, filt_ref, order_ref, row_ref, back_ref, pts, wup, wdown, roll_ref, last_ref, msg, own, halo_out, halo_in, t_ref, w_ref, x_ref, d_ref, e_ref, z_ref,
            f_ref, acc_ref, ex_ref, back, pieces, turn_ref, c_ref, load_sem, send_sem, recv_sem, halo_send, halo_recv):
     me = lax.axis_index("lon")
     lat = lax.axis_index("lat")
@@ -341,6 +341,15 @@
     hail(me, lat, lats, barrier)
     fetch_up = pltpu.make_async_copy(wup_hbm, wup, load_sem.at[1])
     fetch_down = pltpu.make_async_copy(wdown_hbm, wdown, load_sem.at[2])
+    tables = [
+        pltpu.make_async_copy(src, dst, load_sem.at[3 + i])
+        for i, (src, dst) in enumerate(
+            ((sup_hbm, sup_ref), (sin_hbm, sin_ref), (filt_hbm, filt_ref), (order_hbm, order_ref), (row_hbm, row_ref),
+             (back_hbm, back_ref))
+        )
+    ]
+    for copy in tables:
+        copy.start()
     fetch_up.start()
     fetch_down.start()
     fetch.wait()
@@ -352,6 +361,8 @@
     send_all(me, msg.at[1], own.at[1], send_sem.at[1], recv_sem.at[1])
     for h in range(2):
         own[h, me] = msg[h, me]
+    for copy in tables:
+        copy.wait()
     build_weights(sup_ref, sin_ref, lat * ROWS, t_ref)
     build_filter(filt_ref, me, w_ref)
     for step in range(9):
@@ -434,8 +445,7 @@
 
 
 VM = pl.BlockSpec(memory_space=pltpu.VMEM)
-SM = pl.BlockSpec(memory_space=pltpu.SMEM)
-ANY = pl.BlockSpec(memory_space=pl.ANY)
+HBM = pl.BlockSpec(memory_space=pltpu.HBM)
 
 
 def on_device(lats, fields, support, filter_weight, w_up, w_down):
@@ -443,8 +453,10 @@
     dma = pltpu.SemaphoreType.DMA
     result = pl.pallas_call(
         functools.partial(kernel, lats), out_shape=jax.ShapeDtypeStruct((NB, ROWS, C), BF),
-        in_specs=[ANY, SM, SM, VM, VM, VM, VM, ANY, ANY], out_specs=VM,
+        in_specs=[HBM] * 9, out_specs=VM,
         scratch_shapes=[
+            pltpu.SMEM((5, 180), jnp.int32), pltpu.SMEM((1, 192), F32), pltpu.VMEM((K, C), BF),
+            pltpu.VMEM((2, 2, 64, 128), BF), pltpu.VMEM((128, 128), BF), pltpu.VMEM((2, 2, 48, 384), BF),
             pltpu.VMEM((NB, ROWS, C), BF), pltpu.VMEM(w_up.shape, BF), pltpu.VMEM(w_up.shape, BF),
             pltpu.VMEM((NB, 16, 768), F32), pltpu.VMEM((3, 8, 128), F32),
             pltpu.VMEM((2, OWN, 8, 128), BF), pltpu.VMEM((2, OWN, 8, 128), BF),
@@ -455,12 +467,13 @@
             pltpu.VMEM((9, 320, 384), BF), pltpu.VMEM((256, 384), F32), pltpu.VMEM((16, OWN, 128), F32),
             pltpu.VMEM((2, OWN, 8, 128), BF), pltpu.VMEM((2, OWN, 8, 128), BF),
             pltpu.VMEM((2 * OWN, 16, 128), F32), pltpu.VMEM((192, 768), F32),
-            dma((3,)), dma((4,)), dma((4,)), dma((2, 2)), dma((2, 2)),
+            dma((9,)), dma((4,)), dma((4,)), dma((2, 2)), dma((2, 2)),
         ],
-        compiler_params=pltpu.CompilerParams(vmem_limit_bytes=60 << 20, collective_id=0, has_side_effects=True),
+        compiler_params=pltpu.CompilerParams(vmem_limit_bytes=40 << 20, collective_id=0, has_side_effects=True),
         name="block",
-    )(points, support.T, jnp.asarray(sines()), filter_weight.T, jnp.asarray(order_matrix(), BF),
-      jnp.asarray(row_matrix(), BF), jnp.asarray(back_matrix(), BF), w_up, w_down.T)
+    )(*(pltpu.with_memory_space_constraint(x, pltpu.HBM) for x in (
+        points, support.T, jnp.asarray(sines()), filter_weight.T, jnp.asarray(order_matrix(), BF),
+        jnp.asarray(row_matrix(), BF), jnp.asarray(back_matrix(), BF), w_up, w_down.T)))
     return jnp.transpose(result, (1, 2, 0))
 
 

time: 64.3 us -> 61.6 us (0.958)
  Pallas kernels: 62.4 us -> 60.8 us
  local copies, waits for them, and re-layouts: 1.69 us -> 0.72 us
    pallas_call x1, Pallas kernels: 62.4 us -> 60.8 us  [on_device(): pl.pallas_call(functools.partial(kernel, lats), out_shape=jax.ShapeDtypeS...]
    unnamed x1, local copies, waits for them, and re-layouts: 1.69 us -> 0.72 us
where the time goes in v3:
time: 61.6 us; the launch traced here: 61.5 us
  Pallas kernels  60.8 us (99%)
  local copies, waits for them, and re-layouts  0.72 us (1%)
    pallas_call x1, Pallas kernels, on_device(): pl.pallas_call(functools.partial(kernel, lats), out_shape=jax.ShapeDtypeS...  60.8 us

profile of v3, /device:TPU:193, one launch (start us, length us, event | category | flops | bytes accessed | tf_op | source)
XLA Modules:
  0.0 61.5 jit_solution(8568616824273202804)
XLA Ops:
  0.0 60.8 %block.1 = bf16[12,15,641]{2,1,0:T(8,128)(2,1)S(1)} custom-call(bf16[12,15,641]{2,1,0:T(8,128)(2,1)} %bitcast.7, s32[5,180]{1,0:T(8,128)} %bitcast.8, f32[1,192]{1,0:T(1,128)} %constant.8.clone.sin_hbm, bf16[4,641]{1,0:T(4,128)(2,1)} %bitcast.9, bf16[2,2,64,128]{3,2,1,0:T(8,128)(2,1)} %constant.9.clone.order_hbm, bf16[128,128]{1,0:T(8,128)(2,1)} %constant.10.clone.row_hbm, ...), custom_call_target="tpu_custom_call" | custom-call | tf_op jit(solution)/shard_map/block/pallas_call | solution.py:454
  60.8 0.7 %copy.11 = bf16[15,641,12]{1,0,2:T(8,128)(2,1)} copy(bf16[15,641,12]{1,0,2:T(8,128)(2,1)S(1)} %bitcast.5) | data formatting | bytes 461520
